TPU v7x, 512 devices: a whole 4x8x8 slice. The times are simulated.
512 devices in a mesh: dp: 16 (over y_hi, x), fsdp: 32 (over z, y_lo, core).
Axes of the slice: x: 4, y: 8 (y_hi: 4, y_lo: 2; y = y_hi * 2 + y_lo), z: 8, core: 2. Of those that a mesh axis runs over, the one named last changes fastest.
Arguments:
- tokens: bfloat16 [65536, 8192], P(('dp', 'fsdp')), may hold values from -6 to 6
- frozen_key_matrix: bfloat16 [8192, 512], P('fsdp'), may hold values from -0.0625 to 0.0625
- adapter_down_factor: float32 [96, 8192, 16], P('fsdp', 'dp'), may hold values from -0.0625 to 0.0625
- adapter_up_factor: float32 [96, 16, 512], P('fsdp', None, 'dp'), may hold values from -1.5 to 1.5
- key_norm_gain: float32 [128], replicated, may hold values from 0.1 to 1.9
- adapter_offset: int32 [16, 32], P('dp', 'fsdp'), may hold values from 0 to 2, as said below
- loss_row_count: int32 [16, 32], P('dp', 'fsdp'), may hold values from 32 to 128, as said below
- cotangent: bfloat16 [65536, 512], P(('dp', 'fsdp')), may hold values from -6 to 6
Outputs:
- keys: bfloat16 [65536, 512], P(('dp', 'fsdp'))
- input_grad: bfloat16 [65536, 8192], P(('dp', 'fsdp'))
- down_grad: float32 [96, 8192, 16], P('fsdp', 'dp')
- up_factor_gradient: float32 [96, 16, 512], P('fsdp', None, 'dp')
Inputs may be any that keep to these rules, and one draw needn't show every extreme that they name: `adapter_offset`: in every column j, each offset 0 to 2 is named by at least one dp index. `loss_row_count`: some block has 128 live rows and some block 32.
All inputs are finite; a program needn't handle non-finite values.
Results may differ from a plain program's by a relative error of at most 0.0033.
Values may be sent and summed in bfloat16 or wider, within the bound.
A program may use at most 64 MiB of HBM per device.

v0:
```python
import jax
import jax.numpy as jnp
from jax import lax
from jax.sharding import PartitionSpec as P

HD = 128
adapter_scale = 2.0
norm_eps = 1e-06


def on_device(
    tokens,
    frozen_key_matrix,
    adapter_down_factor,
    adapter_up_factor,
    key_norm_gain,
    adapter_offset,
    loss_row_count,
    cotangent,
):
    highest_precision = lax.Precision.HIGHEST
    row_count = tokens.shape[0]
    key_width = frozen_key_matrix.shape[1]
    stored_values = adapter_down_factor.shape[0]
    slot_value = adapter_offset[0, 0]
    live_count = loss_row_count[0, 0]
    selector = jnp.arange(stored_values, dtype=jnp.int32) == slot_value
    counted = jnp.where(selector, live_count, 0)
    summed_rows = lax.psum(counted, "dp")
    adapter_total = jnp.sum(jnp.where(selector, summed_rows, 0)).astype(jnp.float32)
    down_whole, up_whole = (
        lax.all_gather(adapter_down_factor, "dp", axis=1, tiled=True),
        lax.all_gather(adapter_up_factor, "dp", axis=2, tiled=True),
    )
    down_projection = lax.dynamic_index_in_dim(down_whole, slot_value, 0, keepdims=False)
    up_projection = lax.dynamic_index_in_dim(up_whole, slot_value, 0, keepdims=False)
    weight = lax.all_gather(frozen_key_matrix, "fsdp", axis=0, tiled=True)
    frozen_output = jnp.dot(tokens, weight, preferred_element_type=jnp.float32)
    tokens_float = tokens.astype(jnp.float32)
    lowrank_output = jnp.dot(tokens_float, down_projection, precision=highest_precision)
    projected_keys = frozen_output + adapter_scale * jnp.dot(
        lowrank_output, up_projection, precision=highest_precision
    )
    shaped = projected_keys.reshape(row_count, -1, HD)
    mean_square = jnp.mean(shaped * shaped, axis=-1, keepdims=True)
    inverse_rms = lax.rsqrt(mean_square + norm_eps)
    normed = shaped * inverse_rms
    keys = (normed * key_norm_gain).reshape(row_count, key_width).astype(jnp.bfloat16)
    row_mask = (jnp.arange(row_count, dtype=jnp.int32) < live_count).astype(jnp.float32)
    row_grad = cotangent.astype(jnp.float32) * row_mask[:, None] * (row_count / adapter_total)
    scaled_grad = row_grad.reshape(normed.shape) * key_norm_gain
    along_norm = jnp.mean(scaled_grad * normed, axis=-1, keepdims=True)
    prenorm_gradient = (inverse_rms * (scaled_grad - normed * along_norm)).reshape(
        row_count, key_width
    )
    pre_grad_low = prenorm_gradient.astype(jnp.bfloat16)
    lowrank_gradient = adapter_scale * jnp.dot(
        prenorm_gradient, up_projection.T, precision=highest_precision
    )
    input_base = lax.dot_general(
        pre_grad_low, weight, (((1,), (1,)), ((), ())), preferred_element_type=jnp.float32
    )
    input_grad = (
        input_base + jnp.dot(lowrank_gradient, down_projection.T, precision=highest_precision)
    ).astype(jnp.bfloat16)
    down_grad = lax.dot_general(
        tokens_float, lowrank_gradient, (((0,), (0,)), ((), ())), precision=highest_precision
    )
    up_factor_gradient = adapter_scale * lax.dot_general(
        lowrank_output, prenorm_gradient, (((0,), (0,)), ((), ())), precision=highest_precision
    )
    selector_float = selector.astype(jnp.float32)
    down_terms = selector_float[:, None, None] * down_grad[None]
    up_terms = selector_float[:, None, None] * up_factor_gradient[None]
    down_sum, up_sum = (
        lax.psum_scatter(down_terms, "dp", scatter_dimension=1, tiled=True),
        lax.psum_scatter(up_terms, "dp", scatter_dimension=2, tiled=True),
    )
    return (keys, input_grad, down_sum, up_sum)


def solution(mesh):
    placed = (
        P(("dp", "fsdp"), None),
        P("fsdp", None),
        P("fsdp", "dp", None),
        P("fsdp", None, "dp"),
        P(),
        P("dp", "fsdp"),
        P("dp", "fsdp"),
        P(("dp", "fsdp"), None),
    )
    return jax.shard_map(
        on_device,
        mesh=mesh,
        in_specs=placed,
        out_specs=(
            P(("dp", "fsdp"), None),
            P(("dp", "fsdp"), None),
            P("fsdp", "dp", None),
            P("fsdp", None, "dp"),
        ),
        check_vma=False,
    )
```

profile of v0, /device:TPU:64, one launch (start us, length us, event | category | flops | bytes accessed | tf_op | source)
XLA Modules:
  0.0 360.2 jit_solution(965696795780993262)
XLA Ops:
  7.2 0.0 copy-start
  7.2 0.0 copy-start.2
  7.2 0.0 all-gather.5.cloned.1.call-start
  7.2 0.7 all-gather.5.cloned.1.call-update
  7.9 0.0 all-gather.3.cloned.1.call-start
  8.0 0.7 all-gather.3.cloned.1.call-update
  8.7 0.0 reduce-scatter.7.cloned.1.call-start
  10.0 18.7 %psum.7 = s32[3]{0:T(128)S(1)} all-reduce(s32[3]{0:T(128)S(1)} %fusion.12), channel_id=1, replica_groups=mesh['dp'=16,'fsdp'=32] {'dp'}, use_global_device_ids=true, to_apply=%region_1.2 | all-reduce | flops 3 | bytes 24 | tf_op jit(solution)/shard_map/psum | solution.py:29
  28.7 0.8 copy.12
  29.5 0.6 select_reduce_fusion
  30.9 1.0 multiply_multiply_fusion
  31.9 0.1 reshape.48
  32.0 55.4 %all_gather.11 = f32[3,16,512]{1,0,2:T(4,128)S(1)} all-gather(f32[3,16,32]{1,0,2:T(4,128)S(1)} %copy.12), channel_id=1, replica_groups=mesh['dp'=16,'fsdp'=32] {'dp'}, dimensions={2}, use_global_device_ids=true | all-gather | bytes 104448 | tf_op jit(solution)/shard_map/all_gather | solution.py:33
  87.4 0.2 constant_dynamic-slice_fusion
  87.6 0.0 copy-done.2
  87.6 0.0 all-gather.5.cloned.1.call-done
  87.6 0.0 copy-done
  87.7 2.8 fusion.3
  90.4 65.8 %all-gather.3.cloned.1.call-done = bf16[8192,512]{1,0:T(8,128)(2,1)} async-done(((bf16[256,512]{1,0:T(8,128)(2,1)}), bf16[8192,512]{1,0:T(8,128)(2,1)}) %all-gather.3.cloned.1.call-update) | async-done | bytes 8388624 | tf_op jit(solution)/shard_map/all_gather | solution.py:37
  156.2 4.6 %fusion.15 = f32[128,512]{1,0:T(8,128)S(1)} fusion(bf16[128,8192]{1,0:T(8,128)(2,1)S(1)} %copy-done, bf16[8192,512]{1,0:T(8,128)(2,1)} %all-gather.3.cloned.1.call-done), kind=kOutput, calls=%fused_computation.35 | convolution fusion | flops 1073741824 | bytes 10747904 | tf_op jit(solution)/shard_map/dot_general | solution.py:38
  160.9 0.0 copy-start.1
  160.9 0.4 fusion.1
  161.3 0.1 reshape.47
  161.4 0.2 multiply_reduce_fusion.1
  161.7 0.4 multiply_reduce_fusion
  162.0 0.2 mul.139
  162.2 0.2 mul.123
  162.4 0.0 copy-done.1
  162.5 0.7 fusion.8
  163.2 0.5 convolution_multiply_fusion.2
  163.7 0.3 convolution_multiply_fusion.1
  164.0 1.7 convolution_bitcast_fusion
  165.7 0.1 broadcast_multiply_fusion.1
  165.8 0.4 copy.13
  166.2 1.1 reshape.49
  167.3 0.0 reduce-scatter.7.cloned.1.call-update
  167.3 0.0 reduce-scatter.5.cloned.1.call-start
  167.3 2.4 broadcast_multiply_fusion
  169.7 0.0 reduce-scatter.5.cloned.1.call-update
  169.7 6.2 %fusion.9 = f32[128,8192]{1,0:T(8,128)S(1)} fusion(bf16[8192,512]{1,0:T(8,128)(2,1)} %all-gather.3.cloned.1.call-done, f32[128,512]{1,0:T(8,128)S(1)} %get-tuple-element.4), kind=kOutput, calls=%fused_computation.21 | convolution fusion | flops 1073807360 | bytes 12845056 | tf_op jit(solution)/shard_map/dot_general | solution.py:60
  175.9 5.9 %fusion = bf16[128,8192]{1,0:T(8,128)(2,1)} fusion(f32[128,8192]{1,0:T(8,128)S(1)} %fusion.9, f32[128,16]{0,1:T(8,128)S(1)} %convolution_multiply_fusion.2, f32[3,8192,16]{1,2,0:T(8,128)} %all-gather.5.cloned.1.call-done, s32[]{:T(128)S(6)} %select_n.14), kind=kOutput, calls=%fused_computation.1 | convolution fusion | flops 203423744 | bytes 6823940 | tf_op jit(solution)/shard_map/dot_general | solution.py:64
  181.8 76.3 %reduce-scatter.7.cloned.1.call-done = f32[32,48]{1,0:T(8,128)} async-done(((f32[512,48]{1,0:T(8,128)}), f32[32,48]{1,0:T(8,128)}) %reduce-scatter.7.cloned.1.call-update) | async-done | bytes 6160
  258.1 0.8 reshape.50
  258.9 0.7 copy.14
  259.6 94.1 %reduce-scatter.5.cloned.1.call-done = f32[3,512,16]{1,2,0:T(8,128)} async-done(((f32[3,8192,16]{1,2,0:T(8,128)}), f32[3,512,16]{1,2,0:T(8,128)}) %reduce-scatter.5.cloned.1.call-update) | async-done | bytes 98320 | tf_op jit(solution)/shard_map/reduce_scatter | solution.py:76
  (6 shorter events, 0.0 us)
Async XLA Ops:
  7.2 80.5 %copy-start = (bf16[128,8192]{1,0:T(8,128)(2,1)S(1)}, bf16[128,8192]{1,0:T(8,128)(2,1)}, u32[]{:S(2)}) copy-start(bf16[128,8192]{1,0:T(8,128)(2,1)} %param.8) | copy-start | bytes 6291460
  7.2 80.4 %copy-start.2 = (f32[128]{0:T(128)S(1)}, f32[128]{0:T(128)}, u32[]{:S(2)}) copy-start(f32[128]{0:T(128)} %param.12) | copy-start | bytes 1540
  7.2 80.4 %all-gather.5.cloned.1.call-start = ((), (), s32[]{:S(2)}) async-start(), calls=%async_computation.3 | async-start | bytes 1671168 | tf_op jit(solution)/shard_map/all_gather | solution.py:32
  7.9 148.3 %all-gather.3.cloned.1.call-start = ((), (), s32[]{:S(2)}) async-start(), calls=%async_computation.2 | async-start | bytes 8650752 | tf_op jit(solution)/shard_map/all_gather | solution.py:37
  8.7 249.4 %reduce-scatter.7.cloned.1.call-start = ((), (), s32[]{:S(2)}) async-start(), calls=%async_computation.5 | async-start | bytes 278528
  160.9 1.6 copy-start.1
  167.3 186.4 %reduce-scatter.5.cloned.1.call-start = ((), (), s32[]{:S(2)}) async-start(), calls=%async_computation.4 | async-start | bytes 1671168 | tf_op jit(solution)/shard_map/reduce_scatter | solution.py:76
Sparse Core Ops, SparseCore 0:
  11.0 70.9 all-gather.4
  84.2 72.0 all-gather.2
  167.4 90.6 reduce-scatter.6
  263.2 90.4 reduce-scatter.4
where the time goes:
time: 361 us; the launch traced here: 360 us
  waiting for transfers between devices  238 us (66%)
  blocking collectives  74.1 us (21%)
  matrix products  22.5 us (6%)
  between operations  15.9 us (4%)
  other arithmetic  5.37 us (1%)
  local copies, waits for them, and re-layouts  4.64 us (1%)
    reduce_scatter x1, waiting for transfers between devices, on_device(): lax.psum_scatter(down_terms, 'dp', scatter_dimension=1, tiled=True)  94.1 us
    unnamed x5, waiting for transfers between devices  77.7 us
    all_gather x1, waiting for transfers between devices, on_device(): weight = lax.all_gather(frozen_key_matrix, 'fsdp', axis=0, tiled=True)  65.8 us
    all_gather x1, blocking collectives, on_device(): lax.all_gather(adapter_up_factor, 'dp', axis=2, tiled=True)  55.4 us
    psum x1, blocking collectives, on_device(): summed_rows = lax.psum(counted, 'dp')  18.7 us
  transfers between devices with their start and end apart: 4, of which 3 were waited for; matrix products, arithmetic and copies ran while one was open for 6% of the time, Pallas kernels for 0%

commit v1 on v0

--- a/solution.py
+++ b/solution.py
@@ -6,6 +6,13 @@
 HD = 128
 adapter_scale = 2.0
 norm_eps = 1e-06
+
+
+def all_by_exchange(x, axis, along):
+    n_dev = lax.axis_size(axis)
+    blocks = jnp.stack([x for _ in range(n_dev)])
+    blocks = lax.all_to_all(blocks, axis, split_axis=0, concat_axis=0)
+    return jnp.concatenate(blocks, axis=along)
 
 
 def on_device(
@@ -34,7 +41,7 @@
     )
     down_projection = lax.dynamic_index_in_dim(down_whole, slot_value, 0, keepdims=False)
     up_projection = lax.dynamic_index_in_dim(up_whole, slot_value, 0, keepdims=False)
-    weight = lax.all_gather(frozen_key_matrix, "fsdp", axis=0, tiled=True)
+    weight = all_by_exchange(frozen_key_matrix, "fsdp", 0)
     frozen_output = jnp.dot(tokens, weight, preferred_element_type=jnp.float32)
     tokens_float = tokens.astype(jnp.float32)
     lowrank_output = jnp.dot(tokens_float, down_projection, precision=highest_precision)

time: 361 us -> 447 us (1.24)
  blocking collectives: 74.1 us -> 214 us
  waiting for transfers between devices: 238 us -> 169 us
  starting transfers between devices: 0.16 us -> 11.6 us
  local copies, waits for them, and re-layouts: 4.64 us -> 9.17 us
    psum x1, blocking collectives: 18.7 us -> 159 us  [on_device(): summed_rows = lax.psum(counted, 'dp')]
    all_gather x1 -> x0, waiting for transfers between devices: 65.8 us -> none  [on_device(): weight = lax.all_gather(frozen_key_matrix, 'fsdp', axis=0, tiled=True)]
    all_to_all x0 -> x1, starting transfers between devices: none -> 11.3 us  [all_by_exchange(): blocks = lax.all_to_all(blocks, axis, split_axis=0, concat_axis=0)]
    another operation x0 -> x1, local copies, waits for them, and re-layouts: none -> 5.25 us  [all_by_exchange(): blocks = jnp.stack([x for _ in range(n_dev)])]
    unnamed x5 -> x4, waiting for transfers between devices: 77.7 us -> 75.2 us
  transfers between devices with their start and end apart: 4 -> 4, of which waited for: 3 -> 2; matrix products, arithmetic and copies ran while one was open for 6% -> 4% of each run, Pallas kernels for 0% -> 0%
where the time goes in v1:
time: 447 us
  blocking collectives  214 us (48%)
  waiting for transfers between devices  169 us (38%)
  matrix products  22.4 us (5%)
  between operations  15.9 us (4%)
  starting transfers between devices  11.6 us (3%)
  local copies, waits for them, and re-layouts  9.17 us (2%)
  other arithmetic  4.55 us (1%)
    psum x1, blocking collectives, on_device(): summed_rows = lax.psum(counted, 'dp')  159 us
    reduce_scatter x1, waiting for transfers between devices, on_device(): lax.psum_scatter(down_terms, 'dp', scatter_dimension=1, tiled=True)  94.1 us
    unnamed x4, waiting for transfers between devices  75.2 us
    all_gather x1, blocking collectives, on_device(): lax.all_gather(adapter_up_factor, 'dp', axis=2, tiled=True)  54.3 us
    all_to_all x1, starting transfers between devices, all_by_exchange(): blocks = lax.all_to_all(blocks, axis, split_axis=0, concat_axis=0)  11.3 us
  transfers between devices with their start and end apart: 4, of which 2 were waited for; matrix products, arithmetic and copies ran while one was open for 4% of the time, Pallas kernels for 0%

profile of v1, /device:TPU:64, one launch (start us, length us, event | category | flops | bytes accessed | tf_op | source)
XLA Modules:
  0.0 446.8 jit_solution(6314250162842084171)
XLA Ops:
  7.2 0.0 copy-start
  7.2 5.3 %stack.2 = bf16[32,256,512]{2,1,0:T(8,128)(2,1)} broadcast(bf16[256,512]{1,0:T(8,128)(2,1)} %param.9), dimensions={1,2} | broadcast | bytes 8650752 | tf_op jit(solution)/shard_map/stack | solution.py:13
  12.4 0.0 copy-start.2
  12.4 0.0 copy-start.1
  12.4 11.3 %all-to-all-start = ((bf16[32,256,512]{2,1,0:T(8,128)(2,1)}), bf16[32,256,512]{2,1,0:T(8,128)(2,1)}, u32[]{:S(2)}, u32[]{:S(2)}) async-start(bf16[32,256,512]{2,1,0:T(8,128)(2,1)} %stack.2), calls=%async_computation | async-start | bytes 16777216 | tf_op jit(solution)/shard_map/all_to_all | solution.py:14
  23.8 0.0 copy-start.3
  23.8 0.0 all-gather.2.cloned.1.call-start
  23.8 0.7 all-gather.2.cloned.1.call-update
  24.5 0.0 reduce-scatter.7.cloned.1.call-start
  25.9 159.4 %psum.7 = s32[3]{0:T(128)S(1)} all-reduce(s32[3]{0:T(128)S(1)} %fusion.12), channel_id=1, replica_groups=mesh['dp'=16,'fsdp'=32] {'dp'}, use_global_device_ids=true, to_apply=%region_1.2 | all-reduce | flops 3 | bytes 24 | tf_op jit(solution)/shard_map/psum | solution.py:36
  185.3 0.0 copy-done.2
  185.3 0.1 copy.12
  185.4 0.6 select_reduce_fusion
  186.7 0.0 copy-done.1
  186.7 0.1 multiply_multiply_fusion
  186.8 0.1 reshape.54
  186.9 54.3 %all_gather.7 = f32[3,16,512]{1,0,2:T(4,128)S(1)} all-gather(f32[3,16,32]{1,0,2:T(4,128)S(1)} %copy.12), channel_id=1, replica_groups=mesh['dp'=16,'fsdp'=32] {'dp'}, dimensions={2}, use_global_device_ids=true | all-gather | bytes 104448 | tf_op jit(solution)/shard_map/all_gather | solution.py:40
  241.2 0.2 constant_dynamic-slice_fusion
  241.4 0.0 copy-done.3
  241.5 0.0 all-gather.2.cloned.1.call-done
  241.5 0.0 copy-done
  241.5 2.8 fusion.3
  244.3 0.0 all-to-all-done
  244.3 4.6 %fusion.15 = f32[128,512]{1,0:T(8,128)S(1)} fusion(bf16[128,8192]{1,0:T(8,128)(2,1)S(1)} %copy-done, bf16[8192,512]{1,0:T(8,128)(2,1)} %bitcast), kind=kOutput, calls=%fused_computation.35 | convolution fusion | flops 1073741824 | bytes 10747904 | tf_op jit(solution)/shard_map/dot_general | solution.py:45
  248.9 0.4 fusion.1
  249.4 0.1 reshape.53
  249.5 0.2 multiply_reduce_fusion.1
  249.7 0.4 multiply_reduce_fusion
  250.1 0.2 mul.139
  250.3 0.2 mul.123
  250.5 0.7 fusion.8
  251.2 0.5 convolution_multiply_fusion.2
  251.7 0.3 convolution_multiply_fusion.1
  252.0 1.7 convolution_bitcast_fusion
  253.7 0.1 broadcast_multiply_fusion.1
  253.8 0.4 copy.13
  254.2 1.1 reshape.55
  255.3 0.0 reduce-scatter.7.cloned.1.call-update
  255.3 0.2 reduce-scatter.5.cloned.1.call-start
  255.6 2.4 broadcast_multiply_fusion
  258.0 0.0 reduce-scatter.5.cloned.1.call-update
  258.0 6.2 %fusion.9 = f32[128,8192]{1,0:T(8,128)S(1)} fusion(bf16[8192,512]{1,0:T(8,128)(2,1)} %bitcast, f32[128,512]{1,0:T(8,128)S(1)} %get-tuple-element.4), kind=kOutput, calls=%fused_computation.21 | convolution fusion | flops 1073807360 | bytes 12845056 | tf_op jit(solution)/shard_map/dot_general | solution.py:67
  264.2 5.9 %fusion = bf16[128,8192]{1,0:T(8,128)(2,1)} fusion(f32[128,8192]{1,0:T(8,128)S(1)} %fusion.9, f32[128,16]{0,1:T(8,128)S(1)} %convolution_multiply_fusion.2, f32[3,8192,16]{1,2,0:T(8,128)} %all-gather.2.cloned.1.call-done, s32[]{:T(128)S(6)} %select_n.14), kind=kOutput, calls=%fused_computation.1 | convolution fusion | flops 203423744 | bytes 6823940 | tf_op jit(solution)/shard_map/dot_general | solution.py:71
  270.1 74.5 %reduce-scatter.7.cloned.1.call-done = f32[32,48]{1,0:T(8,128)} async-done(((f32[512,48]{1,0:T(8,128)}), f32[32,48]{1,0:T(8,128)}) %reduce-scatter.7.cloned.1.call-update) | async-done | bytes 6160
  344.6 0.8 reshape.56
  345.5 0.7 copy.14
  346.2 94.1 %reduce-scatter.5.cloned.1.call-done = f32[3,512,16]{1,2,0:T(8,128)} async-done(((f32[3,8192,16]{1,2,0:T(8,128)}), f32[3,512,16]{1,2,0:T(8,128)}) %reduce-scatter.5.cloned.1.call-update) | async-done | bytes 98320 | tf_op jit(solution)/shard_map/reduce_scatter | solution.py:83
  (6 shorter events, 0.0 us)
Async XLA Ops:
  7.2 234.3 %copy-start = (bf16[128,8192]{1,0:T(8,128)(2,1)S(1)}, bf16[128,8192]{1,0:T(8,128)(2,1)}, u32[]{:S(2)}) copy-start(bf16[128,8192]{1,0:T(8,128)(2,1)} %param.8) | copy-start | bytes 6291460
  12.4 172.8 %copy-start.2 = (f32[3,16,32]{2,1,0:T(8,128)S(1)}, f32[3,16,32]{2,1,0:T(8,128)}, u32[]{:S(2)}) copy-start(f32[3,16,32]{2,1,0:T(8,128)} %param.11) | copy-start | bytes 18436
  12.4 174.3 %copy-start.1 = (bf16[128,512]{1,0:T(8,128)(2,1)S(1)}, bf16[128,512]{1,0:T(8,128)(2,1)}, u32[]{:S(2)}) copy-start(bf16[128,512]{1,0:T(8,128)(2,1)} %param.15) | copy-start | bytes 393220
  12.4 231.9 %all-to-all-start = ((bf16[32,256,512]{2,1,0:T(8,128)(2,1)}), bf16[32,256,512]{2,1,0:T(8,128)(2,1)}, u32[]{:S(2)}, u32[]{:S(2)}) async-start(bf16[32,256,512]{2,1,0:T(8,128)(2,1)} %stack.2), calls=%async_computation | async-start | bytes 16777216 | tf_op jit(solution)/shard_map/all_to_all | solution.py:14
  23.8 217.7 %copy-start.3 = (f32[128]{0:T(128)S(1)}, f32[128]{0:T(128)}, u32[]{:S(2)}) copy-start(f32[128]{0:T(128)} %param.12) | copy-start | bytes 1540
  23.8 217.7 %all-gather.2.cloned.1.call-start = ((), (), s32[]{:S(2)}) async-start(), calls=%async_computation.3 | async-start | bytes 1671168 | tf_op jit(solution)/shard_map/all_gather | solution.py:39
  24.5 320.1 %reduce-scatter.7.cloned.1.call-start = ((), (), s32[]{:S(2)}) async-start(), calls=%async_computation.5 | async-start | bytes 278528
  255.3 184.9 %reduce-scatter.5.cloned.1.call-start = ((), (), s32[]{:S(2)}) async-start(), calls=%async_computation.4 | async-start | bytes 1671168 | tf_op jit(solution)/shard_map/reduce_scatter | solution.py:83
Sparse Core Ops, SparseCore 0:
  27.6 73.3 all-gather.1
  255.5 89.1 reduce-scatter.6
  349.9 90.2 reduce-scatter.4
